TPU v7x, 32 devices: a whole 2x2x4 slice. The times are simulated.
32 devices in a mesh: seq: 8 (over z, y), head: 4 (over x, core).
Axes of the slice: x: 2, y: 2, z: 4, core: 2. Of those that a mesh axis runs over, the one named last changes fastest.
Arguments:
- tokens: bfloat16 [2048, 1024], P('seq'), may hold values from -6 to 6
- w_qkv: bfloat16 [1024, 3, 1024], P('seq', None, 'head'), may hold values from -0.1875 to 0.1875
- w_out: bfloat16 [1024, 1024], P('head', 'seq'), may hold values from -1 to 1
- ln1_gain: bfloat16 [1024], P('seq'), may hold values from 0.5 to 1.5
- ln1_bias: bfloat16 [1024], P('seq'), may hold values from -1.796875 to 1.796875
- ln2_gain: bfloat16 [1024], P('seq'), may hold values from 0.5 to 1.5
- ln2_bias: bfloat16 [1024], P('seq'), may hold values from -1.796875 to 1.796875
- w_up: bfloat16 [1024, 4096], P('seq', 'head'), may hold values from -0.1875 to 0.1875
- up_bias: bfloat16 [4096], P('head'), may hold values from -1.796875 to 1.796875
- w_down: bfloat16 [4096, 1024], P('head', 'seq'), may hold values from -0.09375 to 0.09375
- down_bias: bfloat16 [1024], P('seq'), may hold values from -1.796875 to 1.796875
- seq_units: int32 [4], replicated, may hold values from 1 to 4, 8 in all
- seq_pad: int32 [4], replicated, may hold values from 0 to 127
- rand_picks: int32 [32, 16, 3], P('seq', 'head'), may hold values from 0 to 65535
- cotangent: bfloat16 [2048, 1024], P('seq'), may hold values from -6 to 6
Outputs:
- output: bfloat16 [2048, 1024], P('seq')
- x_grad: float32 [2048, 1024], P('seq')
- w_qkv_grad: float32 [1024, 3, 1024], P('seq', None, 'head')
- w_out_grad: float32 [1024, 1024], P('head', 'seq')
- ln1_gain_grad: float32 [1024], P('seq')
- ln1_bias_grad: float32 [1024], P('seq')
- ln2_gain_grad: float32 [1024], P('seq')
- ln2_bias_grad: float32 [1024], P('seq')
- w_up_grad: float32 [1024, 4096], P('seq', 'head')
- up_bias_grad: float32 [4096], P('head')
- w_down_grad: float32 [4096, 1024], P('head', 'seq')
- down_bias_grad: float32 [1024], P('seq')
Inputs may be any that keep to these rules, and one draw needn't show every extreme that they name: `seq_units`: each sequence covers whole units; the values add up to the number of units in the stream, and some sequence covers 4 units.
All inputs are finite; a program needn't handle non-finite values.
Results may differ from a plain program's by a relative error of at most 0.012.
Values may be sent and summed in bfloat16 or wider, within the bound.
A program may use at most 128 MiB of HBM per device.

v0:
```python
import jax
import jax.numpy as jnp
from jax import lax
from jax.sharding import PartitionSpec as P

HEAD_DIM = 64
BLK = 64
SPAN = 4
BLK_DEV = 4
EPSILON = 1e-05
NEGATIVE = -1e30
F32 = jnp.float32
BF16 = jnp.bfloat16


def shifted(value, axis, steps):
    count = lax.axis_size(axis)
    first, last = (max(0, -steps), min(count, count - steps))
    return lax.ppermute(value, axis, [(i, i + steps) for i in range(first, last)])


def norm_parts(features):
    average = jnp.mean(features, axis=-1, keepdims=True)
    centred = features - average
    spread = jnp.mean(centred * centred, axis=-1, keepdims=True)
    inverse = lax.rsqrt(spread + EPSILON)
    return (centred * inverse, inverse)


def norm_backward(xhat, inverse, scaled):
    first = jnp.mean(scaled, axis=-1, keepdims=True)
    second = jnp.mean(scaled * xhat, axis=-1, keepdims=True)
    return inverse * (scaled - first - xhat * second)


def dot(a, b, dims):
    return lax.dot_general(a, b, (dims, ((), ())), preferred_element_type=F32)


def sequence_place(seq_units, seq_pad):
    device = lax.axis_index("seq")
    start, leader, span, pad = (0, 0, 0, 0)
    for k in range(seq_units.shape[0]):
        units = seq_units[k]
        inside = (device >= start) & (device < start + units)
        leader = jnp.where(inside, start, leader)
        span = jnp.where(inside, units, span)
        pad = jnp.where(inside, seq_pad[k], pad)
        start = start + units
    return (device - leader, span, pad)


def key_counts(position, span, picks):
    blocks = lax.broadcasted_iota(jnp.int32, (1, 1, SPAN * BLK_DEV), 2)
    query = position * BLK_DEV + lax.broadcasted_iota(jnp.int32, (BLK_DEV, 1, 1), 0)
    total = span * BLK_DEV
    count = jnp.zeros((BLK_DEV, picks.shape[1], SPAN * BLK_DEV), F32)
    for wanted in (query - 1, query, query + 1, 0, total - 1):
        count = count + (blocks == wanted).astype(F32)
    chosen = picks % total
    for r in range(picks.shape[2]):
        count = count + (blocks == chosen[:, :, r : r + 1]).astype(F32)
    return jnp.where((query == 0) | (query == total - 1), 1.0, count)


def local_general(
    tokens,
    w_qkv,
    w_out,
    ln1_gain,
    ln1_bias,
    ln2_gain,
    ln2_bias,
    w_up,
    up_bias,
    w_down,
    down_bias,
    seq_units,
    seq_pad,
    rand_picks,
    cotangent,
):
    tok, width = tokens.shape
    heads = w_qkv.shape[2] // HEAD_DIM
    rows = lambda v: lax.all_gather(v, "seq", axis=0, tiled=True)
    cols = lambda v: lax.all_gather(v, "seq", axis=1, tiled=True)
    vectors = jnp.stack([ln1_gain, ln1_bias, ln2_gain, ln2_bias, down_bias], axis=0)
    gain_one, shift_one, gain_two, shift_two, down_shift = [
        v[None].astype(F32) for v in cols(vectors)
    ]
    qkv = rows(w_qkv)
    out_w, up_w, down_w = (cols(w_out), rows(w_up), cols(w_down))
    position, span, pad = sequence_place(seq_units, seq_pad)
    root = SPAN - 1 - position
    inputs = tokens.astype(F32)
    xhat_one, inv_one = norm_parts(inputs)
    normed = (xhat_one * gain_one + shift_one).astype(BF16)
    triple = jnp.einsum("td,dcf->tcf", normed, qkv, preferred_element_type=F32).astype(BF16)
    own = jnp.stack([triple[:, 1], triple[:, 2]], axis=0)
    pieces = [own if o == 0 else shifted(own, "seq", -o) for o in range(1 - SPAN, SPAN)]
    nearby = jnp.stack(pieces, axis=0)
    window = lax.dynamic_slice_in_dim(nearby, root, SPAN, 0)
    split = lambda v: v.reshape(v.shape[0], heads, HEAD_DIM)
    keys = split(window[:, 0].reshape(SPAN * tok, -1))
    values = split(window[:, 1].reshape(SPAN * tok, -1))
    queries = split(triple[:, 0])
    scaling = HEAD_DIM ** (-0.5)
    live = jnp.arange(SPAN * tok, dtype=jnp.int32) < span * tok - pad
    count = jnp.repeat(key_counts(position, span, rand_picks), BLK, axis=2)
    count = jnp.where(live[None, None], count, 0.0)
    count = jnp.transpose(jnp.repeat(count, BLK, axis=0), (1, 0, 2))
    logits = jnp.einsum("qhd,khd->hqk", queries, keys, preferred_element_type=F32) * scaling
    logits = jnp.where(count > 0, logits, NEGATIVE)
    grown = jnp.exp(logits - jnp.max(logits, axis=-1, keepdims=True)) * count
    chances = grown / jnp.sum(grown, axis=-1, keepdims=True)
    chances_low = chances.astype(BF16)
    attended = jnp.einsum("hqk,khd->qhd", chances_low, values, preferred_element_type=F32)
    attended = attended.astype(BF16).reshape(tok, heads * HEAD_DIM)
    middle = inputs + lax.psum(dot(attended, out_w, ((1,), (0,))), "head")
    xhat_two, inv_two = norm_parts(middle)
    normed_two = (xhat_two * gain_two + shift_two).astype(BF16)
    pre_act = dot(normed_two, up_w, ((1,), (0,))) + up_bias.astype(F32)[None]
    hidden, pull = jax.vjp(lambda v: jax.nn.gelu(v, approximate=True), pre_act)
    hidden = hidden.astype(BF16)
    ffn = lax.psum(dot(hidden, down_w, ((1,), (0,))).astype(BF16), "head").astype(F32)
    output = (middle + ffn + down_shift).astype(BF16)
    grad_out = cotangent.astype(F32)
    grad_w_down = dot(hidden, cotangent, ((0,), (0,)))
    grad_pre = pull(dot(cotangent, down_w, ((1,), (1,))))[0].astype(BF16)
    grad_w_up = dot(normed_two, grad_pre, ((0,), (0,)))
    grad_up_bias = lax.psum(jnp.sum(grad_pre.astype(F32), axis=0), "seq")
    grad_two = lax.psum(dot(grad_pre, up_w, ((1,), (1,))), "head")
    grad_middle = grad_out + norm_backward(xhat_two, inv_two, grad_two * gain_two)
    grad_branch = grad_middle.astype(BF16)
    grad_w_out = dot(attended, grad_branch, ((0,), (0,)))
    grad_att = split(dot(grad_branch, out_w, ((1,), (1,))).astype(BF16))
    grad_prob = jnp.einsum("qhd,khd->hqk", grad_att, values, preferred_element_type=F32)
    inner = jnp.sum(chances * grad_prob, axis=-1, keepdims=True)
    grad_logit = (chances * (grad_prob - inner)).astype(BF16)
    dq = scaling * jnp.einsum("hqk,khd->qhd", grad_logit, keys, preferred_element_type=F32)
    dk = scaling * jnp.einsum("hqk,qhd->khd", grad_logit, queries, preferred_element_type=F32)
    dv = jnp.einsum("hqk,qhd->khd", chances_low, grad_att, preferred_element_type=F32)
    part = jnp.stack([dk.reshape(SPAN, tok, -1), dv.reshape(SPAN, tok, -1)], axis=1)
    near = jnp.zeros((2 * SPAN - 1,) + part.shape[1:], F32)
    near = lax.dynamic_update_slice_in_dim(near, part, root, 0)
    owned = near[SPAN - 1]
    for offset in range(1 - SPAN, SPAN):
        if offset:
            owned = owned + shifted(near[offset + SPAN - 1], "seq", offset)
    owned = owned.astype(BF16)
    grad_triple = jnp.stack([dq.reshape(tok, -1).astype(BF16), owned[0], owned[1]], axis=1)
    grad_w_qkv = jnp.einsum("td,tcf->dcf", normed, grad_triple, preferred_element_type=F32)
    grad_one = lax.psum(
        jnp.einsum("tcf,dcf->td", grad_triple, qkv, preferred_element_type=F32), "head"
    )
    x_grad = grad_middle + norm_backward(xhat_one, inv_one, grad_one * gain_one)
    sums = jnp.stack(
        [
            jnp.sum(grad_one * xhat_one, axis=0),
            jnp.sum(grad_one, axis=0),
            jnp.sum(grad_two * xhat_two, axis=0),
            jnp.sum(grad_two, axis=0),
            jnp.sum(grad_out, axis=0),
        ],
        axis=0,
    )
    scatter = lambda v, d: lax.psum_scatter(v, "seq", scatter_dimension=d, tiled=True)
    sums = scatter(sums, 1)
    return (
        output,
        x_grad,
        scatter(grad_w_qkv, 0),
        scatter(grad_w_out, 1),
        sums[0],
        sums[1],
        sums[2],
        sums[3],
        scatter(grad_w_up, 0),
        grad_up_bias,
        scatter(grad_w_down, 1),
        sums[4],
    )


IN_SPECS = (
    P("seq", None),
    P("seq", None, "head"),
    P("head", "seq"),
    P("seq"),
    P("seq"),
    P("seq"),
    P("seq"),
    P("seq", "head"),
    P("head"),
    P("head", "seq"),
    P("seq"),
    P(),
    P(),
    P("seq", "head", None),
    P("seq", None),
)
OUT_SPECS = (
    P("seq", None),
    P("seq", None),
    P("seq", None, "head"),
    P("head", "seq"),
    P("seq"),
    P("seq"),
    P("seq"),
    P("seq"),
    P("seq", "head"),
    P("head"),
    P("head", "seq"),
    P("seq"),
)


def solution(mesh):
    return jax.shard_map(
        local_general, mesh=mesh, in_specs=IN_SPECS, out_specs=OUT_SPECS, check_vma=False
    )
```

profile of v0, /device:TPU:0, one launch (start us, length us, event | category | flops | bytes accessed | tf_op | source)
XLA Modules:
  0.0 851.5 jit_solution(9352380124314227854)
XLA Ops:
  23.5 27.9 %all_gather.15 = bf16[5,1024]{1,0:T(8,128)(2,1)S(1)} all-gather(bf16[5,128]{1,0:T(8,128)(2,1)S(1)} %stack.75), channel_id=1, replica_groups=mesh['seq'=8,'head'=4] {'seq'}, dimensions={1}, use_global_device_ids=true | all-gather | bytes 11520 | tf_op jit(solution)/shard_map/all_gather | solution.py:86
  54.2 27.8 %all_gather.17 = bf16[256,1024]{1,0:T(8,128)(2,1)S(1)} all-gather(bf16[256,128]{1,0:T(8,128)(2,1)} %param.17), channel_id=1, replica_groups=mesh['seq'=8,'head'=4] {'seq'}, dimensions={1}, use_global_device_ids=true | all-gather | bytes 589824 | tf_op jit(solution)/shard_map/all_gather | solution.py:86
  86.1 5.1 collective-permute-start.1
  96.8 4.2 collective-permute-done.3
  101.0 6.9 collective-permute-done.4
  109.7 2.9 fusion.49
  113.3 3.2 convolution_convert_fusion.3
  119.3 38.9 %all-reduce.5.cloned.1.call-done = f32[256,1024]{1,0:T(8,128)} async-done(((f32[256,1024]{1,0:T(8,128)}), f32[256,1024]{1,0:T(8,128)}) %all-reduce.5.cloned.1.call-update) | async-done | bytes 1048592 | tf_op jit(solution)/shard_map/psum | solution.py:119
  159.9 52.1 %all-gather.8.cloned.1.call-done = bf16[1024,1024]{1,0:T(8,128)(2,1)} async-done(((bf16[1024,128]{1,0:T(8,128)(2,1)}), bf16[1024,1024]{1,0:T(8,128)(2,1)}) %all-gather.8.cloned.1.call-update) | async-done | bytes 2097168 | tf_op jit(solution)/shard_map/all_gather | solution.py:86
  211.9 3.3 fusion.51
  215.2 46.4 %all-gather.6.cloned.1.call-done = bf16[1024,1024]{1,0:T(8,128)(2,1)} async-done(((bf16[128,1024]{1,0:T(8,128)(2,1)}), bf16[1024,1024]{1,0:T(8,128)(2,1)}) %all-gather.6.cloned.1.call-update) | async-done | bytes 2097168 | tf_op jit(solution)/shard_map/all_gather | solution.py:85
  261.6 3.5 convert_reduce_fusion.2
  267.8 3.2 convolution_convert_fusion
  271.2 31.2 %all-reduce.9.cloned.1.call-done = f32[256,1024]{1,0:T(8,128)} async-done(((f32[256,1024]{1,0:T(8,128)}), f32[256,1024]{1,0:T(8,128)}) %all-reduce.9.cloned.1.call-update) | async-done | bytes 1048592 | tf_op jit(solution)/shard_map/psum | solution.py:132
  304.2 34.6 %all-reduce.7.cloned.1.call-done = bf16[256,1024]{1,0:T(8,128)(2,1)} async-done(((bf16[256,1024]{1,0:T(8,128)(2,1)}), bf16[256,1024]{1,0:T(8,128)(2,1)}) %all-reduce.7.cloned.1.call-update) | async-done | bytes 524304 | tf_op jit(solution)/shard_map/psum | solution.py:125
  338.8 2.9 convert_add_fusion.1
  363.6 4.2 collective-permute-start.10
  367.8 4.3 collective-permute-start.11
  375.9 3.4 collective-permute-done.10
  379.3 4.2 collective-permute-start.9
  384.4 11.5 %collective-permute-done.11 = f32[2,256,256]{2,1,0:T(8,128)} collective-permute-done((f32[2,256,256]{2,1,0:T(8,128)}, f32[2,256,256]{2,1,0:T(8,128)}, u32[]{:S(2)}, u32[]{:S(2)}) %collective-permute-start.11) | collective-permute-done | bytes 524320 | tf_op jit(solution)/shard_map/ppermute | solution.py:19
  395.9 5.4 collective-permute-done.7
  401.3 10.7 %collective-permute-done.9 = f32[2,256,256]{2,1,0:T(8,128)} collective-permute-done((f32[2,256,256]{2,1,0:T(8,128)}, f32[2,256,256]{2,1,0:T(8,128)}, u32[]{:S(2)}, u32[]{:S(2)}) %collective-permute-start.9) | collective-permute-done | bytes 524320 | tf_op jit(solution)/shard_map/ppermute | solution.py:19
  415.9 41.7 %all-reduce.11.cloned.1.call-done = f32[256,1024]{1,0:T(8,128)} async-done(((f32[256,1024]{1,0:T(8,128)}), f32[256,1024]{1,0:T(8,128)}) %all-reduce.11.cloned.1.call-update) | async-done | bytes 1048592 | tf_op jit(solution)/shard_map/psum | solution.py:153
  465.0 2.8 fusion.43
  469.2 2.9 fusion.42
  472.1 22.1 %psum.39 = f32[1024]{0:T(1024)} all-reduce(f32[1024]{0:T(1024)S(1)} %get-tuple-element.20), channel_id=1, replica_groups=mesh['seq'=8,'head'=4] {'seq'}, use_global_device_ids=true, to_apply=%region_25.26 | all-reduce | flops 1024 | bytes 8192 | tf_op jit(solution)/shard_map/psum | solution.py:131
  495.5 19.4 %reduce-scatter.10.cloned.1.call-done = f32[5,128]{1,0:T(8,128)} async-done(((f32[5,1024]{1,0:T(8,128)}), f32[5,128]{1,0:T(8,128)}) %reduce-scatter.10.cloned.1.call-update) | async-done | bytes 2576 | tf_op jit(solution)/shard_map/reduce_scatter | solution.py:167
  516.3 65.9 %reduce-scatter.8.cloned.1.call-done = f32[256,128]{1,0:T(8,128)} async-done(((f32[256,1024]{1,0:T(8,128)}), f32[256,128]{1,0:T(8,128)}) %reduce-scatter.8.cloned.1.call-update) | async-done | bytes 131088 | tf_op jit(solution)/shard_map/reduce_scatter | solution.py:167
  582.2 78.2 %reduce-scatter.6.cloned.1.call-done = f32[128,3,256]{2,0,1:T(8,128)} async-done(((f32[1024,3,256]{2,0,1:T(8,128)}), f32[128,3,256]{2,0,1:T(8,128)}) %reduce-scatter.6.cloned.1.call-update) | async-done | bytes 393232 | tf_op jit(solution)/shard_map/reduce_scatter | solution.py:167
  660.4 91.4 %reduce-scatter.12.cloned.1.call-done = f32[128,1024]{1,0:T(8,128)} async-done(((f32[1024,1024]{1,0:T(8,128)}), f32[128,1024]{1,0:T(8,128)}) %reduce-scatter.12.cloned.1.call-update) | async-done | bytes 524304 | tf_op jit(solution)/shard_map/reduce_scatter | solution.py:167
  751.8 92.8 %reduce-scatter.14.cloned.1.call-done = f32[1024,128]{1,0:T(8,128)} async-done(((f32[1024,1024]{1,0:T(8,128)}), f32[1024,128]{1,0:T(8,128)}) %reduce-scatter.14.cloned.1.call-update) | async-done | bytes 524304 | tf_op jit(solution)/shard_map/reduce_scatter | solution.py:167
  (156 shorter events, 71.9 us)
Async XLA Ops:
  7.2 74.8 %copy-start = (bf16[256,1024]{1,0:T(8,128)(2,1)S(1)}, bf16[256,1024]{1,0:T(8,128)(2,1)}, u32[]{:S(2)}) copy-start(bf16[256,1024]{1,0:T(8,128)(2,1)} %param.15) | copy-start | bytes 1572868
  7.2 74.8 %all-gather.4.cloned.1.call-start = ((), (), s32[]{:S(2)}) async-start(), calls=%async_computation.5 | async-start | bytes 1769472 | tf_op jit(solution)/shard_map/all_gather | solution.py:85
  9.0 149.2 %all-reduce.5.cloned.1.call-start = ((), (), s32[]{:S(2)}) async-start(), calls=%async_computation.6 | async-start | bytes 2097152 | tf_op jit(solution)/shard_map/psum | solution.py:119
  84.2 11.1 %collective-permute-start = (bf16[2,256,256]{1,2,0:T(8,128)(2,1)S(1)}, bf16[2,256,256]{1,2,0:T(8,128)(2,1)S(1)}, u32[]{:S(2)}, u32[]{:S(2)}) collective-permute-start(bf16[2,256,256]{1,2,0:T(8,128)(2,1)S(1)} %pad_maximum_fusion.1), channel_id=1, source_target_pairs={{0,12},{4,16},{8,20},{12,24},{16,28},{1,13},{5,17},{9,21},{13,25},... | collective-permute-start | bytes 786440 | tf_op jit(solution)/shard_map/ppermute | solution.py:19
  86.1 10.6 %collective-permute-start.1 = (bf16[2,256,256]{1,2,0:T(8,128)(2,1)S(1)}, bf16[2,256,256]{1,2,0:T(8,128)(2,1)S(1)}, u32[]{:S(2)}, u32[]{:S(2)}) collective-permute-start(bf16[2,256,256]{1,2,0:T(8,128)(2,1)S(1)} %pad_maximum_fusion.1), channel_id=1, source_target_pairs={{0,8},{4,12},{8,16},{12,20},{16,24},{20,28},{1,9},{5,13},{9,17},{1... | collective-permute-start | bytes 786440 | tf_op jit(solution)/shard_map/ppermute | solution.py:19
  91.3 5.4 collective-permute-start.2
  92.7 8.3 collective-permute-start.3
  94.0 13.9 %collective-permute-start.4 = (bf16[2,256,256]{1,2,0:T(8,128)(2,1)S(1)}, bf16[2,256,256]{1,2,0:T(8,128)(2,1)S(1)}, u32[]{:S(2)}, u32[]{:S(2)}) collective-permute-start(bf16[2,256,256]{1,2,0:T(8,128)(2,1)S(1)} %pad_maximum_fusion.1), channel_id=1, source_target_pairs={{8,0},{12,4},{16,8},{20,12},{24,16},{28,20},{9,1},{13,5},{17,9},{2... | collective-permute-start | bytes 786440 | tf_op jit(solution)/shard_map/ppermute | solution.py:19
  95.3 12.6 %collective-permute-start.5 = (bf16[2,256,256]{1,2,0:T(8,128)(2,1)S(1)}, bf16[2,256,256]{1,2,0:T(8,128)(2,1)S(1)}, u32[]{:S(2)}, u32[]{:S(2)}) collective-permute-start(bf16[2,256,256]{1,2,0:T(8,128)(2,1)S(1)} %pad_maximum_fusion.1), channel_id=1, source_target_pairs={{12,0},{16,4},{20,8},{24,12},{28,16},{13,1},{17,5},{21,9},{25,13},... | collective-permute-start | bytes 786440 | tf_op jit(solution)/shard_map/ppermute | solution.py:19
  117.9 94.0 %copy-start.7 = (bf16[256,1024]{1,0:T(8,128)(2,1)S(1)}, bf16[256,1024]{1,0:T(8,128)(2,1)}, u32[]{:S(2)}) copy-start(bf16[256,1024]{1,0:T(8,128)(2,1)} %param.29) | copy-start | bytes 1572868
  117.9 94.0 %all-gather.8.cloned.1.call-start = ((), (), s32[]{:S(2)}) async-start(), calls=%async_computation.8 | async-start | bytes 2359296 | tf_op jit(solution)/shard_map/all_gather | solution.py:86
  118.6 143.0 %all-gather.6.cloned.1.call-start = ((), (), s32[]{:S(2)}) async-start(), calls=%async_computation.7 | async-start | bytes 2359296 | tf_op jit(solution)/shard_map/all_gather | solution.py:85
  119.2 183.2 %all-reduce.9.cloned.1.call-start = ((), (), s32[]{:S(2)}) async-start(), calls=%async_computation.10 | async-start | bytes 2097152 | tf_op jit(solution)/shard_map/psum | solution.py:132
  261.6 4.3 copy-start.12
  267.7 71.1 %all-reduce.7.cloned.1.call-start = ((), (), s32[]{:S(2)}) async-start(), calls=%async_computation.9 | async-start | bytes 1048576 | tf_op jit(solution)/shard_map/psum | solution.py:125
  271.0 186.6 %all-reduce.11.cloned.1.call-start = ((), (), s32[]{:S(2)}) async-start(), calls=%async_computation.11 | async-start | bytes 2097152 | tf_op jit(solution)/shard_map/psum | solution.py:153
  338.8 3.3 copy-start.19
  360.6 22.9 %copy-start.2 = (bf16[4,256,1024]{2,1,0:T(8,128)(2,1)S(1)}, bf16[4,256,1024]{2,1,0:T(8,128)(2,1)}, u32[]{:S(2)}) copy-start(bf16[4,256,1024]{2,1,0:T(8,128)(2,1)} %copy-done.1) | copy-start | bytes 6291460
  360.6 22.9 %copy-start.6 = (bf16[1024,4,64]{0,2,1:T(8,128)(2,1)S(1)}, bf16[1024,4,64]{0,2,1:T(8,128)(2,1)}, u32[]{:S(2)}) copy-start(bf16[1024,4,64]{0,2,1:T(8,128)(2,1)} %copy-done.5) | copy-start | bytes 1572868
  363.6 15.7 %collective-permute-start.10 = (f32[2,256,256]{2,1,0:T(8,128)S(1)}, f32[2,256,256]{2,1,0:T(8,128)}, u32[]{:S(2)}, u32[]{:S(2)}) collective-permute-start(f32[2,256,256]{2,1,0:T(8,128)S(1)} %get-tuple-element.26), channel_id=1, source_target_pairs={{0,8},{4,12},{8,16},{12,20},{16,24},{20,28},{1,9},{5,13},{9,17},{1... | collective-permute-start | bytes 1572872 | tf_op jit(solution)/shard_map/ppermute | solution.py:19
  367.8 28.1 %collective-permute-start.11 = (f32[2,256,256]{2,1,0:T(8,128)}, f32[2,256,256]{2,1,0:T(8,128)}, u32[]{:S(2)}, u32[]{:S(2)}) collective-permute-start(f32[2,256,256]{2,1,0:T(8,128)} %get-tuple-element.25), channel_id=1, source_target_pairs={{0,12},{4,16},{8,20},{12,24},{16,28},{1,13},{5,17},{9,21},{13,25},... | collective-permute-start | bytes 1572872 | tf_op jit(solution)/shard_map/ppermute | solution.py:19
  372.1 23.9 %collective-permute-start.6 = (f32[2,256,256]{2,1,0:T(8,128)}, f32[2,256,256]{2,1,0:T(8,128)}, u32[]{:S(2)}, u32[]{:S(2)}) collective-permute-start(f32[2,256,256]{2,1,0:T(8,128)} %get-tuple-element.24), channel_id=1, source_target_pairs={{12,0},{16,4},{20,8},{24,12},{28,16},{13,1},{17,5},{21,9},{25,13},... | collective-permute-start | bytes 1572872 | tf_op jit(solution)/shard_map/ppermute | solution.py:19
  373.3 28.0 %collective-permute-start.7 = (f32[2,256,256]{2,1,0:T(8,128)}, f32[2,256,256]{2,1,0:T(8,128)}, u32[]{:S(2)}, u32[]{:S(2)}) collective-permute-start(f32[2,256,256]{2,1,0:T(8,128)} %get-tuple-element.29), channel_id=1, source_target_pairs={{8,0},{12,4},{16,8},{20,12},{24,16},{28,20},{9,1},{13,5},{17,9},{2... | collective-permute-start | bytes 1572872 | tf_op jit(solution)/shard_map/ppermute | solution.py:19
  374.6 26.7 %collective-permute-start.8 = (f32[2,256,256]{2,1,0:T(8,128)}, f32[2,256,256]{2,1,0:T(8,128)}, u32[]{:S(2)}, u32[]{:S(2)}) collective-permute-start(f32[2,256,256]{2,1,0:T(8,128)} %get-tuple-element.28), channel_id=1, source_target_pairs={{4,0},{8,4},{12,8},{16,12},{20,16},{24,20},{28,24},{5,1},{9,5},{13... | collective-permute-start | bytes 1572872 | tf_op jit(solution)/shard_map/ppermute | solution.py:19
  379.3 32.7 %collective-permute-start.9 = (f32[2,256,256]{2,1,0:T(8,128)}, f32[2,256,256]{2,1,0:T(8,128)}, u32[]{:S(2)}, u32[]{:S(2)}) collective-permute-start(f32[2,256,256]{2,1,0:T(8,128)} %get-tuple-element.27), channel_id=1, source_target_pairs={{0,4},{4,8},{8,12},{12,16},{16,20},{20,24},{24,28},{1,5},{5,9},{9,... | collective-permute-start | bytes 1572872 | tf_op jit(solution)/shard_map/ppermute | solution.py:19
  384.4 29.9 %copy-start.15 = (bf16[1024,3,256]{0,2,1:T(8,128)(2,1)S(1)}, bf16[1024,3,256]{0,2,1:T(8,128)(2,1)}, u32[]{:S(2)}) copy-start(bf16[1024,3,256]{0,2,1:T(8,128)(2,1)} %all-gather.4.cloned.1.call-done) | copy-start | bytes 4718596
  415.9 99.1 %reduce-scatter.10.cloned.1.call-start = ((), (), s32[]{:S(2)}) async-start(), calls=%async_computation.14 | async-start | bytes 36864 | tf_op jit(solution)/shard_map/reduce_scatter | solution.py:167
  460.0 122.2 %reduce-scatter.8.cloned.1.call-start = ((), (), s32[]{:S(2)}) async-start(), calls=%async_computation.13 | async-start | bytes 1179648 | tf_op jit(solution)/shard_map/reduce_scatter | solution.py:167
  461.4 199.0 %reduce-scatter.6.cloned.1.call-start = ((), (), s32[]{:S(2)}) async-start(), calls=%async_computation.12 | async-start | bytes 3538944 | tf_op jit(solution)/shard_map/reduce_scatter | solution.py:167
  464.0 287.9 %reduce-scatter.12.cloned.1.call-start = ((), (), s32[]{:S(2)}) async-start(), calls=%async_computation.15 | async-start | bytes 4718592 | tf_op jit(solution)/shard_map/reduce_scatter | solution.py:167
  467.8 376.8 %reduce-scatter.14.cloned.1.call-start = ((), (), s32[]{:S(2)}) async-start(), calls=%async_computation.16 | async-start | bytes 4718592 | tf_op jit(solution)/shard_map/reduce_scatter | solution.py:167
  472.1 22.1 %copy-start.9 = (f32[256,1024]{1,0:T(8,128)S(1)}, f32[256,1024]{1,0:T(8,128)}, u32[]{:S(2)}) copy-start(f32[256,1024]{1,0:T(8,128)} %all-reduce.11.cloned.1.call-done) | copy-start | bytes 3145732
  (13 other events, 24.0 us)
Sparse Core Ops, SparseCore 0:
  10.6 48.0 all-gather.3
  118.0 40.1 all-reduce.4
  160.5 51.4 all-gather.7
  214.1 47.4 all-gather.5
  267.8 34.5 all-reduce.8
  305.2 33.5 all-reduce.6
  416.0 41.5 all-reduce.10
  461.0 53.8 reduce-scatter.9
  519.3 62.8 reduce-scatter.7
  586.3 74.0 reduce-scatter.5
  664.6 87.1 reduce-scatter.11
  756.3 88.2 reduce-scatter.13
where the time goes:
time: 853 us; the launch traced here: 851 us
  waiting for transfers between devices  636 us (75%)
  blocking collectives  77.8 us (9%)
  matrix products  35.6 us (4%)
  starting transfers between devices  29.3 us (3%)
  local copies, waits for them, and re-layouts  29.2 us (3%)
  between operations  24.6 us (3%)
  other arithmetic  18.9 us (2%)
    reduce_scatter x5, waiting for transfers between devices, local_general(): lax.psum_scatter(v, 'seq', scatter_dimension=d, tiled=True)  348 us
    all_gather x2, blocking collectives, local_general(): cols = lambda v: lax.all_gather(v, 'seq', axis=1, tiled=True)  55.7 us
    all_gather x1, waiting for transfers between devices, local_general(): cols = lambda v: lax.all_gather(v, 'seq', axis=1, tiled=True)  52.1 us
    all_gather x2, waiting for transfers between devices, local_general(): rows = lambda v: lax.all_gather(v, 'seq', axis=0, tiled=True)  46.4 us
    ppermute x12, waiting for transfers between devices, shifted(): lax.ppermute(value, axis, [(i, i + steps) for i in range(first, last)])  42.2 us
    psum x1, waiting for transfers between devices, local_general(): lax.psum(jnp.einsum('tcf,dcf->td', grad_triple, qkv, preferred_element_ty...  41.7 us
    psum x1, waiting for transfers between devices, local_general(): middle = inputs + lax.psum(dot(attended, out_w, ((1,), (0,))), 'head')  38.9 us
    psum x1, waiting for transfers between devices, local_general(): lax.psum(dot(hidden, down_w, ((1,), (0,))).astype(BF16), 'head').astype(F32)  34.6 us
  transfers between devices with their start and end apart: 24, of which 17 were waited for; matrix products, arithmetic and copies ran while one was open for 4% of the time, Pallas kernels for 0%

commit v1 on v0

--- a/solution.py
+++ b/solution.py
@@ -116,7 +116,7 @@
     chances_low = chances.astype(BF16)
     attended = jnp.einsum("hqk,khd->qhd", chances_low, values, preferred_element_type=F32)
     attended = attended.astype(BF16).reshape(tok, heads * HEAD_DIM)
-    middle = inputs + lax.psum(dot(attended, out_w, ((1,), (0,))), "head")
+    middle = inputs + jnp.sum(lax.all_gather(dot(attended, out_w, ((1,), (0,))), "head"), axis=0)
     xhat_two, inv_two = norm_parts(middle)
     normed_two = (xhat_two * gain_two + shift_two).astype(BF16)
     pre_act = dot(normed_two, up_w, ((1,), (0,))) + up_bias.astype(F32)[None]

time: 853 us -> 815 us (0.955)
  waiting for transfers between devices: 636 us -> 597 us
    all_gather x1, waiting for transfers between devices: 52.1 us -> 3.45 us  [local_general(): cols = lambda v: lax.all_gather(v, 'seq', axis=1, tiled=True)]
    all_gather x0 -> x1, waiting for transfers between devices: none -> 40.4 us  [local_general(): lax.all_gather(dot(attended, out_w, ((1,), (0,))), 'head')]
    psum x1 -> x0, waiting for transfers between devices: 38.9 us -> none  [local_general(): middle = inputs + lax.psum(dot(attended, out_w, ((1,), (0,))), 'head')]
  transfers between devices with their start and end apart: 24 -> 24, of which waited for: 17 -> 18; matrix products, arithmetic and copies ran while one was open for 4% -> 5% of each run, Pallas kernels for 0% -> 0%
where the time goes in v1:
time: 815 us; the launch traced here: 814 us
  waiting for transfers between devices  597 us (73%)
  blocking collectives  79.2 us (10%)
  matrix products  35.6 us (4%)
  starting transfers between devices  29 us (4%)
  local copies, waits for them, and re-layouts  28.4 us (3%)
  between operations  24.6 us (3%)
  other arithmetic  20.4 us (3%)
    reduce_scatter x5, waiting for transfers between devices, local_general(): lax.psum_scatter(v, 'seq', scatter_dimension=d, tiled=True)  347 us
    all_gather x2, blocking collectives, local_general(): cols = lambda v: lax.all_gather(v, 'seq', axis=1, tiled=True)  57.1 us
    ppermute x12, waiting for transfers between devices, shifted(): lax.ppermute(value, axis, [(i, i + steps) for i in range(first, last)])  48.6 us
    all_gather x2, waiting for transfers between devices, local_general(): rows = lambda v: lax.all_gather(v, 'seq', axis=0, tiled=True)  48.2 us
    psum x1, waiting for transfers between devices, local_general(): lax.psum(jnp.einsum('tcf,dcf->td', grad_triple, qkv, preferred_element_ty...  41.7 us
    all_gather x1, waiting for transfers between devices, local_general(): lax.all_gather(dot(attended, out_w, ((1,), (0,))), 'head')  40.4 us
    psum x1, waiting for transfers between devices, local_general(): lax.psum(dot(hidden, down_w, ((1,), (0,))).astype(BF16), 'head').astype(F32)  34.8 us
    psum x1, waiting for transfers between devices, local_general(): grad_two = lax.psum(dot(grad_pre, up_w, ((1,), (1,))), 'head')  31.2 us
  transfers between devices with their start and end apart: 24, of which 18 were waited for; matrix products, arithmetic and copies ran while one was open for 5% of the time, Pallas kernels for 0%

profile of v1, /device:TPU:0, one launch (start us, length us, event | category | flops | bytes accessed | tf_op | source)
XLA Modules:
  0.0 813.8 jit_solution(13401661254692145176)
XLA Ops:
  19.2 28.0 %all_gather.21 = bf16[5,1024]{1,0:T(8,128)(2,1)S(1)} all-gather(bf16[5,128]{1,0:T(8,128)(2,1)S(1)} %stack.75), channel_id=1, replica_groups=mesh['seq'=8,'head'=4] {'seq'}, dimensions={1}, use_global_device_ids=true | all-gather | bytes 11520 | tf_op jit(solution)/shard_map/all_gather | solution.py:86
  52.1 29.1 %all_gather.23 = bf16[256,1024]{1,0:T(8,128)(2,1)S(1)} all-gather(bf16[256,128]{1,0:T(8,128)(2,1)S(1)} %copy-done.20), channel_id=1, replica_groups=mesh['seq'=8,'head'=4] {'seq'}, dimensions={1}, use_global_device_ids=true | all-gather | bytes 589824 | tf_op jit(solution)/shard_map/all_gather | solution.py:86
  87.2 3.6 collective-permute-start.1
  90.8 3.1 collective-permute-start.2
  97.9 8.9 %collective-permute-done.2 = bf16[2,256,256]{1,2,0:T(8,128)(2,1)S(1)} collective-permute-done((bf16[2,256,256]{1,2,0:T(8,128)(2,1)S(1)}, bf16[2,256,256]{1,2,0:T(8,128)(2,1)S(1)}, u32[]{:S(2)}, u32[]{:S(2)}) %collective-permute-start.2) | collective-permute-done | bytes 262176 | tf_op jit(solution)/shard_map/ppermute | solution.py:19
  108.1 7.4 collective-permute-done.4
  117.2 2.9 fusion.49
  120.8 3.2 convolution_convert_fusion.3
  126.1 3.4 all-gather.10.cloned.1.call-done
  129.5 3.3 fusion.51
  132.8 40.4 %all-gather.12.cloned.1.call-done = f32[1024,1024]{1,0:T(8,128)} async-done(((f32[256,1024]{1,0:T(8,128)}), f32[1024,1024]{1,0:T(8,128)}) %all-gather.12.cloned.1.call-update) | async-done | bytes 4194320 | tf_op jit(solution)/shard_map/all_gather | solution.py:119
  176.5 48.1 %all-gather.8.cloned.1.call-done = bf16[1024,1024]{1,0:T(8,128)(2,1)} async-done(((bf16[128,1024]{1,0:T(8,128)(2,1)}), bf16[1024,1024]{1,0:T(8,128)(2,1)}) %all-gather.8.cloned.1.call-update) | async-done | bytes 2097168 | tf_op jit(solution)/shard_map/all_gather | solution.py:85
  224.6 3.5 convert_reduce_fusion.2
  230.7 3.2 convolution_convert_fusion
  234.1 31.2 %all-reduce.6.cloned.1.call-done = f32[256,1024]{1,0:T(8,128)} async-done(((f32[256,1024]{1,0:T(8,128)}), f32[256,1024]{1,0:T(8,128)}) %all-reduce.6.cloned.1.call-update) | async-done | bytes 1048592 | tf_op jit(solution)/shard_map/psum | solution.py:132
  267.0 34.8 %all-reduce.4.cloned.1.call-done = bf16[256,1024]{1,0:T(8,128)(2,1)} async-done(((bf16[256,1024]{1,0:T(8,128)(2,1)}), bf16[256,1024]{1,0:T(8,128)(2,1)}) %all-reduce.4.cloned.1.call-update) | async-done | bytes 524304 | tf_op jit(solution)/shard_map/psum | solution.py:125
  301.8 2.9 convert_add_fusion.1
  326.6 4.2 collective-permute-start.10
  330.8 4.3 collective-permute-start.11
  339.0 3.4 collective-permute-done.10
  342.4 4.2 collective-permute-start.9
  347.4 11.6 %collective-permute-done.11 = f32[2,256,256]{2,1,0:T(8,128)} collective-permute-done((f32[2,256,256]{2,1,0:T(8,128)}, f32[2,256,256]{2,1,0:T(8,128)}, u32[]{:S(2)}, u32[]{:S(2)}) %collective-permute-start.11) | collective-permute-done | bytes 524320 | tf_op jit(solution)/shard_map/ppermute | solution.py:19
  359.0 5.4 collective-permute-done.7
  364.4 10.7 %collective-permute-done.9 = f32[2,256,256]{2,1,0:T(8,128)} collective-permute-done((f32[2,256,256]{2,1,0:T(8,128)}, f32[2,256,256]{2,1,0:T(8,128)}, u32[]{:S(2)}, u32[]{:S(2)}) %collective-permute-start.9) | collective-permute-done | bytes 524320 | tf_op jit(solution)/shard_map/ppermute | solution.py:19
  379.0 41.7 %all-reduce.8.cloned.1.call-done = f32[256,1024]{1,0:T(8,128)} async-done(((f32[256,1024]{1,0:T(8,128)}), f32[256,1024]{1,0:T(8,128)}) %all-reduce.8.cloned.1.call-update) | async-done | bytes 1048592 | tf_op jit(solution)/shard_map/psum | solution.py:153
  432.3 2.9 fusion.42
  435.2 22.1 %psum.31 = f32[1024]{0:T(1024)} all-reduce(f32[1024]{0:T(1024)S(1)} %get-tuple-element.20), channel_id=1, replica_groups=mesh['seq'=8,'head'=4] {'seq'}, use_global_device_ids=true, to_apply=%region_25.26 | all-reduce | flops 1024 | bytes 8192 | tf_op jit(solution)/shard_map/psum | solution.py:131
  458.7 19.0 %reduce-scatter.10.cloned.1.call-done = f32[5,128]{1,0:T(8,128)} async-done(((f32[5,1024]{1,0:T(8,128)}), f32[5,128]{1,0:T(8,128)}) %reduce-scatter.10.cloned.1.call-update) | async-done | bytes 2576 | tf_op jit(solution)/shard_map/reduce_scatter | solution.py:167
  479.1 65.5 %reduce-scatter.8.cloned.1.call-done = f32[256,128]{1,0:T(8,128)} async-done(((f32[256,1024]{1,0:T(8,128)}), f32[256,128]{1,0:T(8,128)}) %reduce-scatter.8.cloned.1.call-update) | async-done | bytes 131088 | tf_op jit(solution)/shard_map/reduce_scatter | solution.py:167
  544.6 78.4 %reduce-scatter.6.cloned.1.call-done = f32[128,3,256]{2,0,1:T(8,128)} async-done(((f32[1024,3,256]{2,0,1:T(8,128)}), f32[128,3,256]{2,0,1:T(8,128)}) %reduce-scatter.6.cloned.1.call-update) | async-done | bytes 393232 | tf_op jit(solution)/shard_map/reduce_scatter | solution.py:167
  623.0 91.7 %reduce-scatter.12.cloned.1.call-done = f32[128,1024]{1,0:T(8,128)} async-done(((f32[1024,1024]{1,0:T(8,128)}), f32[128,1024]{1,0:T(8,128)}) %reduce-scatter.12.cloned.1.call-update) | async-done | bytes 524304 | tf_op jit(solution)/shard_map/reduce_scatter | solution.py:167
  714.7 92.3 %reduce-scatter.14.cloned.1.call-done = f32[1024,128]{1,0:T(8,128)} async-done(((f32[1024,1024]{1,0:T(8,128)}), f32[1024,128]{1,0:T(8,128)}) %reduce-scatter.14.cloned.1.call-update) | async-done | bytes 524304 | tf_op jit(solution)/shard_map/reduce_scatter | solution.py:167
  (161 shorter events, 75.1 us)
Async XLA Ops:
  7.2 76.2 %copy-start = (bf16[256,1024]{1,0:T(8,128)(2,1)S(1)}, bf16[256,1024]{1,0:T(8,128)(2,1)}, u32[]{:S(2)}) copy-start(bf16[256,1024]{1,0:T(8,128)(2,1)} %param.15) | copy-start | bytes 1572868
  7.2 43.7 %copy-start.21 = (s32[4]{0:T(128)S(1)}, s32[4]{0:T(128)}, u32[]{:S(2)}) copy-start(s32[4]{0:T(128)} %param.27) | copy-start | bytes 52
  7.2 44.9 %copy-start.20 = (bf16[256,128]{1,0:T(8,128)(2,1)S(1)}, bf16[256,128]{1,0:T(8,128)(2,1)}, u32[]{:S(2)}) copy-start(bf16[256,128]{1,0:T(8,128)(2,1)} %param.17) | copy-start | bytes 196612
  7.2 76.2 %all-gather.6.cloned.1.call-start = ((), (), s32[]{:S(2)}) async-start(), calls=%async_computation.5 | async-start | bytes 1769472 | tf_op jit(solution)/shard_map/all_gather | solution.py:85
  9.1 120.5 %all-gather.10.cloned.1.call-start = ((), (), s32[]{:S(2)}) async-start(), calls=%async_computation.7 | async-start | bytes 2359296 | tf_op jit(solution)/shard_map/all_gather | solution.py:86
  9.8 163.4 %all-gather.12.cloned.1.call-start = ((), (), s32[]{:S(2)}) async-start(), calls=%async_computation.16 | async-start | bytes 5242880 | tf_op jit(solution)/shard_map/all_gather | solution.py:119
  85.6 10.9 %collective-permute-start = (bf16[2,256,256]{1,2,0:T(8,128)(2,1)S(1)}, bf16[2,256,256]{1,2,0:T(8,128)(2,1)S(1)}, u32[]{:S(2)}, u32[]{:S(2)}) collective-permute-start(bf16[2,256,256]{1,2,0:T(8,128)(2,1)S(1)} %pad_maximum_fusion.1), channel_id=1, source_target_pairs={{0,12},{4,16},{8,20},{12,24},{16,28},{1,13},{5,17},{9,21},{13,25},... | collective-permute-start | bytes 786440 | tf_op jit(solution)/shard_map/ppermute | solution.py:19
  87.2 10.7 %collective-permute-start.1 = (bf16[2,256,256]{1,2,0:T(8,128)(2,1)S(1)}, bf16[2,256,256]{1,2,0:T(8,128)(2,1)S(1)}, u32[]{:S(2)}, u32[]{:S(2)}) collective-permute-start(bf16[2,256,256]{1,2,0:T(8,128)(2,1)S(1)} %pad_maximum_fusion.1), channel_id=1, source_target_pairs={{0,8},{4,12},{8,16},{12,20},{16,24},{20,28},{1,9},{5,13},{9,17},{1... | collective-permute-start | bytes 786440 | tf_op jit(solution)/shard_map/ppermute | solution.py:19
  90.8 15.9 %collective-permute-start.2 = (bf16[2,256,256]{1,2,0:T(8,128)(2,1)S(1)}, bf16[2,256,256]{1,2,0:T(8,128)(2,1)S(1)}, u32[]{:S(2)}, u32[]{:S(2)}) collective-permute-start(bf16[2,256,256]{1,2,0:T(8,128)(2,1)S(1)} %pad_maximum_fusion.1), channel_id=1, source_target_pairs={{0,4},{4,8},{8,12},{12,16},{16,20},{20,24},{24,28},{1,5},{5,9},{9,... | collective-permute-start | bytes 786440 | tf_op jit(solution)/shard_map/ppermute | solution.py:19
  93.9 14.1 %collective-permute-start.3 = (bf16[2,256,256]{1,2,0:T(8,128)(2,1)S(1)}, bf16[2,256,256]{1,2,0:T(8,128)(2,1)S(1)}, u32[]{:S(2)}, u32[]{:S(2)}) collective-permute-start(bf16[2,256,256]{1,2,0:T(8,128)(2,1)S(1)} %pad_maximum_fusion.1), channel_id=1, source_target_pairs={{4,0},{8,4},{12,8},{16,12},{20,16},{24,20},{28,24},{5,1},{9,5},{13... | collective-permute-start | bytes 786440 | tf_op jit(solution)/shard_map/ppermute | solution.py:19
  95.2 20.3 %collective-permute-start.4 = (bf16[2,256,256]{1,2,0:T(8,128)(2,1)S(1)}, bf16[2,256,256]{1,2,0:T(8,128)(2,1)S(1)}, u32[]{:S(2)}, u32[]{:S(2)}) collective-permute-start(bf16[2,256,256]{1,2,0:T(8,128)(2,1)S(1)} %pad_maximum_fusion.1), channel_id=1, source_target_pairs={{8,0},{12,4},{16,8},{20,12},{24,16},{28,20},{9,1},{13,5},{17,9},{2... | collective-permute-start | bytes 786440 | tf_op jit(solution)/shard_map/ppermute | solution.py:19
  96.5 19.0 %collective-permute-start.5 = (bf16[2,256,256]{1,2,0:T(8,128)(2,1)S(1)}, bf16[2,256,256]{1,2,0:T(8,128)(2,1)S(1)}, u32[]{:S(2)}, u32[]{:S(2)}) collective-permute-start(bf16[2,256,256]{1,2,0:T(8,128)(2,1)S(1)} %pad_maximum_fusion.1), channel_id=1, source_target_pairs={{12,0},{16,4},{20,8},{24,12},{28,16},{13,1},{17,5},{21,9},{25,13},... | collective-permute-start | bytes 786440 | tf_op jit(solution)/shard_map/ppermute | solution.py:19
  124.1 5.5 copy-start.7
  125.4 99.1 %all-gather.8.cloned.1.call-start = ((), (), s32[]{:S(2)}) async-start(), calls=%async_computation.6 | async-start | bytes 2359296 | tf_op jit(solution)/shard_map/all_gather | solution.py:85
  126.0 139.3 %all-reduce.6.cloned.1.call-start = ((), (), s32[]{:S(2)}) async-start(), calls=%async_computation.9 | async-start | bytes 2097152 | tf_op jit(solution)/shard_map/psum | solution.py:132
  230.6 71.2 %all-reduce.4.cloned.1.call-start = ((), (), s32[]{:S(2)}) async-start(), calls=%async_computation.8 | async-start | bytes 1048576 | tf_op jit(solution)/shard_map/psum | solution.py:125
  233.9 186.8 %all-reduce.8.cloned.1.call-start = ((), (), s32[]{:S(2)}) async-start(), calls=%async_computation.10 | async-start | bytes 2097152 | tf_op jit(solution)/shard_map/psum | solution.py:153
  323.7 22.9 %copy-start.2 = (bf16[4,256,1024]{2,1,0:T(8,128)(2,1)S(1)}, bf16[4,256,1024]{2,1,0:T(8,128)(2,1)}, u32[]{:S(2)}) copy-start(bf16[4,256,1024]{2,1,0:T(8,128)(2,1)} %copy-done.1) | copy-start | bytes 6291460
  323.7 22.9 %copy-start.6 = (bf16[1024,4,64]{0,2,1:T(8,128)(2,1)S(1)}, bf16[1024,4,64]{0,2,1:T(8,128)(2,1)}, u32[]{:S(2)}) copy-start(bf16[1024,4,64]{0,2,1:T(8,128)(2,1)} %copy-done.5) | copy-start | bytes 1572868
  326.6 15.8 %collective-permute-start.10 = (f32[2,256,256]{2,1,0:T(8,128)S(1)}, f32[2,256,256]{2,1,0:T(8,128)}, u32[]{:S(2)}, u32[]{:S(2)}) collective-permute-start(f32[2,256,256]{2,1,0:T(8,128)S(1)} %get-tuple-element.26), channel_id=1, source_target_pairs={{0,8},{4,12},{8,16},{12,20},{16,24},{20,28},{1,9},{5,13},{9,17},{1... | collective-permute-start | bytes 1572872 | tf_op jit(solution)/shard_map/ppermute | solution.py:19
  330.8 28.2 %collective-permute-start.11 = (f32[2,256,256]{2,1,0:T(8,128)}, f32[2,256,256]{2,1,0:T(8,128)}, u32[]{:S(2)}, u32[]{:S(2)}) collective-permute-start(f32[2,256,256]{2,1,0:T(8,128)} %get-tuple-element.25), channel_id=1, source_target_pairs={{0,12},{4,16},{8,20},{12,24},{16,28},{1,13},{5,17},{9,21},{13,25},... | collective-permute-start | bytes 1572872 | tf_op jit(solution)/shard_map/ppermute | solution.py:19
  335.1 23.9 %collective-permute-start.6 = (f32[2,256,256]{2,1,0:T(8,128)}, f32[2,256,256]{2,1,0:T(8,128)}, u32[]{:S(2)}, u32[]{:S(2)}) collective-permute-start(f32[2,256,256]{2,1,0:T(8,128)} %get-tuple-element.24), channel_id=1, source_target_pairs={{12,0},{16,4},{20,8},{24,12},{28,16},{13,1},{17,5},{21,9},{25,13},... | collective-permute-start | bytes 1572872 | tf_op jit(solution)/shard_map/ppermute | solution.py:19
  336.4 28.0 %collective-permute-start.7 = (f32[2,256,256]{2,1,0:T(8,128)}, f32[2,256,256]{2,1,0:T(8,128)}, u32[]{:S(2)}, u32[]{:S(2)}) collective-permute-start(f32[2,256,256]{2,1,0:T(8,128)} %get-tuple-element.29), channel_id=1, source_target_pairs={{8,0},{12,4},{16,8},{20,12},{24,16},{28,20},{9,1},{13,5},{17,9},{2... | collective-permute-start | bytes 1572872 | tf_op jit(solution)/shard_map/ppermute | solution.py:19
  337.7 26.7 %collective-permute-start.8 = (f32[2,256,256]{2,1,0:T(8,128)}, f32[2,256,256]{2,1,0:T(8,128)}, u32[]{:S(2)}, u32[]{:S(2)}) collective-permute-start(f32[2,256,256]{2,1,0:T(8,128)} %get-tuple-element.28), channel_id=1, source_target_pairs={{4,0},{8,4},{12,8},{16,12},{20,16},{24,20},{28,24},{5,1},{9,5},{13... | collective-permute-start | bytes 1572872 | tf_op jit(solution)/shard_map/ppermute | solution.py:19
  342.4 32.7 %collective-permute-start.9 = (f32[2,256,256]{2,1,0:T(8,128)}, f32[2,256,256]{2,1,0:T(8,128)}, u32[]{:S(2)}, u32[]{:S(2)}) collective-permute-start(f32[2,256,256]{2,1,0:T(8,128)} %get-tuple-element.27), channel_id=1, source_target_pairs={{0,4},{4,8},{8,12},{12,16},{16,20},{20,24},{24,28},{1,5},{5,9},{9,... | collective-permute-start | bytes 1572872 | tf_op jit(solution)/shard_map/ppermute | solution.py:19
  347.4 29.9 %copy-start.15 = (bf16[1024,3,256]{0,2,1:T(8,128)(2,1)S(1)}, bf16[1024,3,256]{0,2,1:T(8,128)(2,1)}, u32[]{:S(2)}) copy-start(bf16[1024,3,256]{0,2,1:T(8,128)(2,1)} %all-gather.6.cloned.1.call-done) | copy-start | bytes 4718596
  378.9 98.8 %reduce-scatter.10.cloned.1.call-start = ((), (), s32[]{:S(2)}) async-start(), calls=%async_computation.13 | async-start | bytes 36864 | tf_op jit(solution)/shard_map/reduce_scatter | solution.py:167
  423.1 121.5 %reduce-scatter.8.cloned.1.call-start = ((), (), s32[]{:S(2)}) async-start(), calls=%async_computation.12 | async-start | bytes 1179648 | tf_op jit(solution)/shard_map/reduce_scatter | solution.py:167
  424.5 198.5 %reduce-scatter.6.cloned.1.call-start = ((), (), s32[]{:S(2)}) async-start(), calls=%async_computation.11 | async-start | bytes 3538944 | tf_op jit(solution)/shard_map/reduce_scatter | solution.py:167
  427.1 287.6 %reduce-scatter.12.cloned.1.call-start = ((), (), s32[]{:S(2)}) async-start(), calls=%async_computation.14 | async-start | bytes 4718592 | tf_op jit(solution)/shard_map/reduce_scatter | solution.py:167
  430.9 376.0 %reduce-scatter.14.cloned.1.call-start = ((), (), s32[]{:S(2)}) async-start(), calls=%async_computation.15 | async-start | bytes 4718592 | tf_op jit(solution)/shard_map/reduce_scatter | solution.py:167
  435.2 22.1 %copy-start.9 = (f32[256,1024]{1,0:T(8,128)S(1)}, f32[256,1024]{1,0:T(8,128)}, u32[]{:S(2)}) copy-start(f32[256,1024]{1,0:T(8,128)} %all-reduce.8.cloned.1.call-done) | copy-start | bytes 3145732
  (15 other events, 30.8 us)
Sparse Core Ops, SparseCore 0:
  10.7 48.5 all-gather.5
  61.3 68.1 all-gather.9
  131.1 42.1 all-gather.11
  175.3 49.2 all-gather.7
  230.7 34.5 all-reduce.5
  268.2 33.5 all-reduce.3
  379.0 41.5 all-reduce.7
  423.8 53.8 reduce-scatter.9
  481.7 62.8 reduce-scatter.7
  549.1 73.8 reduce-scatter.5
  627.6 87.0 reduce-scatter.11
  718.8 88.1 reduce-scatter.13
